TPU v7x, 512 devices: a whole 4x4x16 slice. The times are simulated.
512 devices in a mesh: segment: 16 (over z_lo, x), dp: 8 (over y, core), mp: 4 (over z_hi).
Axes of the slice: x: 4, y: 4, z: 16 (z_hi: 4, z_lo: 4; z = z_hi * 4 + z_lo), core: 2. Of those that a mesh axis runs over, the one named last changes fastest.
Arguments:
- encoder_image_states: bfloat16 [8, 128, 8192], P('dp', 'segment'), may hold values from -6 to 6
- frozen_key_value: bfloat16 [16, 8192, 2, 1024], P('segment', 'dp', None, 'mp'), may hold values from -0.0625 to 0.0625
- adapter_down_weight: bfloat16 [16, 8192, 128], P('segment', 'mp'), may hold values from -0.0625 to 0.0625
- adapter_up_weight: bfloat16 [16, 2, 64, 1024], P('segment', None, None, 'mp'), may hold values from -0.75 to 0.75
- queries: bfloat16 [16, 8, 128, 8192], P('segment', 'dp', None, 'mp'), may hold values from -9 to 9
- cotangent: bfloat16 [16, 8, 128, 8192], P('segment', 'dp', None, 'mp'), may hold values from -1.5 to 1.5
- text_token_length: int32 [8], P('dp'), may hold values from 32 to 128
- image_tile_count: int32 [8], P('dp'), may hold values from 1 to 4
Outputs:
- grad_down: bfloat16 [16, 8192, 128], P('segment', 'mp')
- up_gradient: bfloat16 [16, 2, 64, 1024], P('segment', None, None, 'mp')
- grad_image: float32 [8, 128, 8192], P('dp', 'segment')
All inputs are finite; a program needn't handle non-finite values.
Results may differ from a plain program's by a relative error of at most 0.017.
The roundings to bfloat16 on the way count: a program that leaves them out, or rounds other values in their place, can miss the bound.
Values may be sent and summed in bfloat16 or wider, within the bound.
No kernel may reach another device: no remote copies, remote signals or barrier semaphores. Data moves between devices by JAX's collectives and lax.ppermute only.
A program may use at most 64 MiB of HBM per device.

v0:
```python
import jax
import jax.numpy as jnp
from jax import lax
from jax.sharding import PartitionSpec as P

HD = 128
TILES = 4
adapter_scale = 2.0
contract_rows = (((0,), (0,)), ((), ()))
contracted_columns = (((1,), (1,)), ((), ()))


def body(
    encoder_image_states,
    frozen_key_value,
    adapter_down_weight,
    adapter_up_weight,
    queries,
    cotangent,
    text_token_length,
    image_tile_count,
):
    samples = encoder_image_states.shape[0]
    model_width = encoder_image_states.shape[2]
    whole_img = lax.all_gather(encoder_image_states, "segment", axis=1, tiled=True)
    image_rows = whole_img.shape[1]
    flat_rows = samples * image_rows
    flat_img = whole_img.reshape(flat_rows, model_width)
    fourth_part = adapter_down_weight.shape[1]
    parallel_index = lax.axis_index("mp")
    image_fourth = lax.dynamic_slice_in_dim(flat_img, parallel_index * fourth_part, fourth_part, 1)
    lowrank_state = adapter_up_weight.shape[2]
    key_value_columns = adapter_up_weight.shape[3]
    lowrank_projection = lax.psum(
        jnp.dot(image_fourth, adapter_down_weight[0], preferred_element_type=jnp.float32), "mp"
    ).astype(jnp.bfloat16)
    adapted_weight = jnp.concatenate(
        [
            jnp.dot(
                lowrank_projection[:, :lowrank_state],
                adapter_up_weight[0, 0],
                preferred_element_type=jnp.float32,
            ),
            jnp.dot(
                lowrank_projection[:, lowrank_state:],
                adapter_up_weight[0, 1],
                preferred_element_type=jnp.float32,
            ),
        ],
        axis=1,
    )
    local_weight = frozen_key_value[0]
    full_weight = lax.all_gather(local_weight, "dp", axis=0, tiled=True).reshape(
        model_width, 2 * key_value_columns
    )
    frozen_output = jnp.dot(flat_img, full_weight, preferred_element_type=jnp.float32)
    key_value_pair = (frozen_output + adapter_scale * adapted_weight).astype(jnp.bfloat16)
    local_heads = queries.shape[3] // HD
    local_kv = key_value_columns // HD
    group_size = local_heads // local_kv
    text_rows = queries.shape[2]
    query_rows = queries[0].reshape(samples, text_rows, local_kv, group_size, HD)
    cot_rows = cotangent[0].reshape(samples, text_rows, local_kv, group_size, HD)
    key_rows = key_value_pair[:, :key_value_columns].reshape(samples, image_rows, local_kv, HD)
    value_rows = key_value_pair[:, key_value_columns:].reshape(samples, image_rows, local_kv, HD)
    key_mask = jnp.arange(image_rows, dtype=jnp.int32)[None, :] < image_tile_count[:, None] * (
        image_rows // TILES
    )
    row_mask = (
        jnp.arange(text_rows, dtype=jnp.int32)[None, :] < text_token_length[:, None]
    ).astype(jnp.float32)
    scores = jnp.einsum(
        "btgrd,bjgd->bgrtj", query_rows, key_rows, preferred_element_type=jnp.float32
    ) * HD ** (-0.5)
    masked = jnp.where(key_mask[:, None, None, None, :], scores, -1e30)
    row_top = jnp.max(masked, axis=-1, keepdims=True)
    shifted = jnp.exp(masked - row_top)
    attention = shifted / jnp.sum(shifted, axis=-1, keepdims=True)
    row_gate = row_mask[:, None, None, :, None]
    kept = attention.astype(jnp.bfloat16) * row_gate.astype(jnp.bfloat16)
    dweights = jnp.einsum(
        "btgrd,bjgd->bgrtj", cot_rows, value_rows, preferred_element_type=jnp.float32
    )
    row_delta = jnp.sum(attention * dweights, axis=-1, keepdims=True)
    dscore = (attention * (dweights - row_delta) * row_gate * HD ** (-0.5)).astype(jnp.bfloat16)
    key_grad = jnp.einsum(
        "bgrtj,btgrd->bjgd", dscore, query_rows, preferred_element_type=jnp.float32
    )
    value_grad = jnp.einsum("bgrtj,btgrd->bjgd", kept, cot_rows, preferred_element_type=jnp.float32)
    kv_grad = jnp.concatenate(
        [
            key_grad.reshape(flat_rows, key_value_columns),
            value_grad.reshape(flat_rows, key_value_columns),
        ],
        axis=1,
    ).astype(jnp.bfloat16)
    backward_piece = adapter_scale * jnp.concatenate(
        [
            lax.dot_general(
                kv_grad[:, :key_value_columns],
                adapter_up_weight[0, 0],
                contracted_columns,
                preferred_element_type=jnp.float32,
            ),
            lax.dot_general(
                kv_grad[:, key_value_columns:],
                adapter_up_weight[0, 1],
                contracted_columns,
                preferred_element_type=jnp.float32,
            ),
        ],
        axis=1,
    )
    backward_lowrank = lax.psum(backward_piece, "mp").astype(jnp.bfloat16)
    up_gradient = adapter_scale * jnp.stack(
        [
            lax.dot_general(
                lowrank_projection[:, :lowrank_state],
                kv_grad[:, :key_value_columns],
                contract_rows,
                preferred_element_type=jnp.float32,
            ),
            lax.dot_general(
                lowrank_projection[:, lowrank_state:],
                kv_grad[:, key_value_columns:],
                contract_rows,
                preferred_element_type=jnp.float32,
            ),
        ]
    )
    grad_down = lax.dot_general(
        image_fourth, backward_lowrank, contract_rows, preferred_element_type=jnp.float32
    )
    down_sum, up_sum = lax.psum((grad_down, up_gradient), "dp")
    image_gradient_total = lax.dot_general(
        kv_grad, full_weight, contracted_columns, preferred_element_type=jnp.float32
    )
    adapter_portion = lax.dot_general(
        backward_lowrank,
        adapter_down_weight[0],
        contracted_columns,
        preferred_element_type=jnp.float32,
    )
    current_layer = lax.dynamic_slice_in_dim(
        image_gradient_total, parallel_index * fourth_part, fourth_part, 1
    )
    image_gradient_total = lax.dynamic_update_slice_in_dim(
        image_gradient_total, current_layer + adapter_portion, parallel_index * fourth_part, 1
    )
    image_gradient_total = image_gradient_total.reshape(samples, image_rows, model_width)
    shared_sum = lax.psum_scatter(image_gradient_total, "segment", scatter_dimension=1, tiled=True)
    result = lax.psum(shared_sum, "mp")
    return (down_sum.astype(jnp.bfloat16)[None], up_sum.astype(jnp.bfloat16)[None], result)


def solution(mesh):
    in_specs = (
        P("dp", "segment", None),
        P("segment", "dp", None, "mp"),
        P("segment", "mp", None),
        P("segment", None, None, "mp"),
        P("segment", "dp", None, "mp"),
        P("segment", "dp", None, "mp"),
        P("dp"),
        P("dp"),
    )
    out_specs = (P("segment", "mp", None), P("segment", None, None, "mp"), P("dp", "segment", None))
    return jax.shard_map(body, mesh=mesh, in_specs=in_specs, out_specs=out_specs, check_vma=False)
```

profile of v0, /device:TPU:2, one launch (start us, length us, event | category | flops | bytes accessed | tf_op | source)
XLA Modules:
  0.0 390.2 jit_solution(4577795114373816345)
XLA Ops:
  7.2 0.7 all-gather.4.cloned.1.call-update
  8.0 0.7 all-gather.6.cloned.1.call-update
  10.0 1.3 copy.38
  11.3 2.0 copy.39
  13.4 88.8 %all-gather.4.cloned.1.call-done = bf16[1,128,8192]{2,1,0:T(8,128)(2,1)} async-done(((bf16[1,8,8192]{2,1,0:T(8,128)(2,1)}), bf16[1,128,8192]{2,1,0:T(8,128)(2,1)}) %all-gather.4.cloned.1.call-update) | async-done | bytes 2097168 | tf_op jit(solution)/shard_map/all_gather | solution.py:25
  102.2 1.3 fusion.21
  103.6 25.9 %psum.35 = bf16[128,128]{1,0:T(8,128)(2,1)S(1)} all-reduce(f32[128,128]{1,0:T(8,128)S(1)} %fusion.21), channel_id=1, replica_groups=mesh['segment'=16,'dp'=8,'mp'=4] {'mp'}, use_global_device_ids=true, to_apply=%region_0.0 | all-reduce | flops 16384 | bytes 98304 | tf_op jit(solution)/shard_map/psum | solution.py:34
  129.5 0.2 fusion.42
  129.7 0.1 fusion.46
  129.8 30.6 %all-gather.6.cloned.1.call-done = bf16[1,8192,2,256]{3,2,0,1:T(2,128)(2,1)} async-done(((bf16[1,1024,2,256]{3,2,0,1:T(2,128)(2,1)}), bf16[1,8192,2,256]{3,2,0,1:T(2,128)(2,1)}) %all-gather.6.cloned.1.call-update) | async-done | bytes 8388624 | tf_op jit(solution)/shard_map/all_gather | solution.py:53
  160.5 8.2 %copy.40 = bf16[1024,8,2,256]{3,1,2,0:T(8,128)(2,1)} copy(bf16[1024,8,2,256]{3,2,1,0:T(2,128)(2,1)} %bitcast.113) | data formatting | bytes 16777216
  168.6 4.6 %fusion.10 = bf16[128,512]{1,0:T(8,128)(2,1)S(1)} fusion(bf16[8192,512]{1,0:T(8,128)(2,1)} %bitcast.108, bf16[1,128,8192]{2,1,0:T(8,128)(2,1)S(1)} %copy-done.1, f32[128,256]{1,0:T(8,128)S(1)} %fusion.42, f32[128,256]{1,0:T(8,128)S(1)} %fusion.46), kind=kOutput, calls=%fused_computation.11 | convolution fusion | flops 1074003968 | bytes 10878976 | tf_op jit(solution)/shard_map/dot_general | solution.py:56
  173.3 0.3 fusion.66
  173.6 0.2 fusion.16
  173.8 1.6 fusion.14
  175.4 0.1 fusion.40
  175.6 0.3 multiply_reduce_fusion
  175.9 0.5 fusion.13
  176.4 1.5 slice-done.1
  177.9 4.8 %fusion.34 = f32[128,8192]{1,0:T(8,128)} fusion(bf16[8192,512]{1,0:T(8,128)(2,1)S(1)} %bitcast.111, bf16[128,256]{0,1:T(8,128)(2,1)S(1)} %bitcast.118, bf16[128,256]{0,1:T(8,128)(2,1)S(1)} %bitcast.120), kind=kOutput, calls=%fused_computation.42 | convolution fusion | flops 1074003968 | bytes 12713984 | tf_op jit(solution)/shard_map/dot_general | solution.py:135
  182.7 0.1 fusion.44
  182.8 26.9 %psum.36 = bf16[128,128]{0,1:T(8,128)(2,1)S(1)} all-reduce(f32[128,128]{0,1:T(8,128)S(1)} %maximum_multiply_fusion.2), channel_id=1, replica_groups=mesh['segment'=16,'dp'=8,'mp'=4] {'mp'}, use_global_device_ids=true, to_apply=%region_4.5 | all-reduce | flops 16384 | bytes 98304 | tf_op jit(solution)/shard_map/psum | solution.py:114
  209.8 4.6 %copy.51 = f32[1,128,8192]{2,1,0:T(8,128)} copy(f32[1,128,8192]{2,1,0:T(8,128)} %bitcast.112) | data formatting | bytes 8388608
  214.3 2.5 fusion.1
  216.8 0.0 all-reduce.4.cloned.1.call-start
  216.9 1.3 fusion.23
  218.2 0.2 convolution_bitcast_fusion.3
  218.4 0.2 convolution_bitcast_fusion.4
  218.7 89.1 %reduce-scatter.2.cloned.1.call-done = f32[1,8,8192]{2,1,0:T(8,128)} async-done(((f32[1,128,8192]{2,1,0:T(8,128)}), f32[1,8,8192]{2,1,0:T(8,128)}) %reduce-scatter.2.cloned.1.call-update) | async-done | bytes 262160 | tf_op jit(solution)/shard_map/reduce_scatter | solution.py:151
  307.7 52.3 %all-reduce.5 = (bf16[2048,128]{1,0:T(8,128)(2,1)}, bf16[2,64,256]{2,1,0:T(8,128)(2,1)}) all-reduce(f32[2048,128]{1,0:T(8,128)} %fusion.23, f32[2,64,256]{2,1,0:T(8,128)S(1)} %maximum_multiply_fusion.1), channel_id=1, replica_groups=mesh['segment'=16,'dp'=8,'mp'=4] {'dp'}, use_global_device_ids=true, to_apply=%region_5.6 | all-reduce | flops 294912 | bytes 1769472 | tf_op jit(solution)/shard_map/psum | solution.py:134
  360.0 22.0 %all-reduce.4.cloned.1.call-done = f32[1,8,8192]{2,1,0:T(8,128)} async-done(((f32[1,8,8192]{2,1,0:T(8,128)}), f32[1,8,8192]{2,1,0:T(8,128)}) %all-reduce.4.cloned.1.call-update) | async-done | bytes 262160 | tf_op jit(solution)/shard_map/psum | solution.py:152
  382.0 1.7 copy.57
  (24 shorter events, 0.3 us)
Async XLA Ops:
  7.2 95.1 %copy-start = (bf16[1,2048,128]{2,1,0:T(8,128)(2,1)S(1)}, bf16[1,2048,128]{2,1,0:T(8,128)(2,1)}, u32[]{:S(2)}) copy-start(bf16[1,2048,128]{2,1,0:T(8,128)(2,1)} %param.10) | copy-start | bytes 1572868
  7.2 122.3 %copy-start.3 = (bf16[1,2,64,256]{3,2,1,0:T(8,128)(2,1)S(1)}, bf16[1,2,64,256]{3,2,1,0:T(8,128)(2,1)}, u32[]{:S(2)}) copy-start(bf16[1,2,64,256]{3,2,1,0:T(8,128)(2,1)} %param.11) | copy-start | bytes 196612
  7.2 95.0 %all-gather.4.cloned.1.call-start = ((), (), s32[]{:S(2)}) async-start(), calls=%async_computation.1 | async-start | bytes 2228224 | tf_op jit(solution)/shard_map/all_gather | solution.py:25
  7.9 152.5 %all-gather.6.cloned.1.call-start = ((), (), s32[]{:S(2)}) async-start(), calls=%async_computation.4 | async-start | bytes 9437184 | tf_op jit(solution)/shard_map/all_gather | solution.py:53
  8.7 299.0 %reduce-scatter.2.cloned.1.call-start = ((), (), s32[]{:S(2)}) async-start(), calls=%async_computation.2 | async-start | bytes 4456448 | tf_op jit(solution)/shard_map/reduce_scatter | solution.py:151
  160.5 8.2 %copy-start.1 = (bf16[1,128,8192]{2,1,0:T(8,128)(2,1)S(1)}, bf16[1,128,8192]{2,1,0:T(8,128)(2,1)}, u32[]{:S(2)}) copy-start(bf16[1,128,8192]{2,1,0:T(8,128)(2,1)} %all-gather.4.cloned.1.call-done) | copy-start | bytes 6291460
  173.3 2.2 copy-start.2
  173.8 2.6 slice-start
  175.6 2.4 slice-start.1
  216.8 165.2 %all-reduce.4.cloned.1.call-start = ((), (), s32[]{:S(2)}) async-start(), calls=%async_computation.3 | async-start | bytes 524288 | tf_op jit(solution)/shard_map/psum | solution.py:152
Sparse Core Ops, SparseCore 0:
  10.1 92.1 all-gather.3
  104.4 56.0 all-gather.5
  217.0 90.7 reduce-scatter.1
  310.5 71.4 all-reduce.3
where the time goes:
time: 391 us; the launch traced here: 390 us
  waiting for transfers between devices  232 us (59%)
  blocking collectives  105 us (27%)
  local copies, waits for them, and re-layouts  19.3 us (5%)
  matrix products  18.3 us (5%)
  between operations  15.2 us (4%)
    reduce_scatter x1, waiting for transfers between devices, body(): lax.psum_scatter(image_gradient_total, 'segment', scatter_dimension=1, ti...  89.1 us
    all_gather x1, waiting for transfers between devices, body(): lax.all_gather(encoder_image_states, 'segment', axis=1, tiled=True)  88.8 us
    psum x1, blocking collectives, body(): down_sum, up_sum = lax.psum((grad_down, up_gradient), 'dp')  52.3 us
    all_gather x1, waiting for transfers between devices, body(): lax.all_gather(local_weight, 'dp', axis=0, tiled=True)  30.6 us
    psum x1, blocking collectives, body(): backward_lowrank = lax.psum(backward_piece, 'mp').astype(jnp.bfloat16)  26.9 us
    psum x1, blocking collectives, body(): lax.psum(jnp.dot(image_fourth, adapter_down_weight[0], preferred_element_...  25.9 us
    psum x1, waiting for transfers between devices, body(): result = lax.psum(shared_sum, 'mp')  22 us
    unnamed x15, local copies, waits for them, and re-layouts  15.9 us
  transfers between devices with their start and end apart: 4, of which 4 were waited for; matrix products, arithmetic and copies ran while one was open for 2% of the time, Pallas kernels for 0%

commit v1 on v0

--- a/solution.py
+++ b/solution.py
@@ -8,6 +8,27 @@
 adapter_scale = 2.0
 contract_rows = (((0,), (0,)), ((), ()))
 contracted_columns = (((1,), (1,)), ((), ()))
+
+
+def collect(shard, axis, dim):
+    count, index, span = (lax.axis_size(axis), lax.axis_index(axis), shard.shape[dim])
+    upward = [(i, (i + 1) % count) for i in range(count)]
+    left = [(i, (i - 1) % count) for i in range(count)]
+    out = jnp.zeros((*shard.shape[:dim], count * span, *shard.shape[dim + 1 :]), shard.dtype)
+    out = lax.dynamic_update_slice_in_dim(out, shard, index * span, axis=dim)
+    from_left = from_right = shard
+    half = count // 2
+    for hop in range(1, half + 1):
+        from_left = lax.ppermute(from_left, axis, upward)
+        out = lax.dynamic_update_slice_in_dim(
+            out, from_left, (index - hop) % count * span, axis=dim
+        )
+        if hop < count - half:
+            from_right = lax.ppermute(from_right, axis, left)
+            out = lax.dynamic_update_slice_in_dim(
+                out, from_right, (index + hop) % count * span, axis=dim
+            )
+    return out
 
 
 def body(
@@ -50,9 +71,7 @@
         axis=1,
     )
     local_weight = frozen_key_value[0]
-    full_weight = lax.all_gather(local_weight, "dp", axis=0, tiled=True).reshape(
-        model_width, 2 * key_value_columns
-    )
+    full_weight = collect(local_weight, "dp", 0).reshape(model_width, 2 * key_value_columns)
     frozen_output = jnp.dot(flat_img, full_weight, preferred_element_type=jnp.float32)
     key_value_pair = (frozen_output + adapter_scale * adapted_weight).astype(jnp.bfloat16)
     local_heads = queries.shape[3] // HD

time: 391 us -> 357 us (0.913)
  waiting for transfers between devices: 232 us -> 173 us
  local copies, waits for them, and re-layouts: 19.3 us -> 41.8 us
  starting transfers between devices: 0.16 us -> 9.1 us
  blocking collectives: 105 us -> 101 us
    all_gather x1, waiting for transfers between devices: 88.8 us -> 34.2 us  [body(): lax.all_gather(encoder_image_states, 'segment', axis=1, tiled=True)]
    all_gather x1 -> x0, waiting for transfers between devices: 30.6 us -> none  [body(): lax.all_gather(local_weight, 'dp', axis=0, tiled=True)]
    ppermute x0 -> x7, waiting for transfers between devices: none -> 25.2 us  [the longest x4 25.2 us: collect(): from_left = lax.ppermute(from_left, axis, upward)]
    dynamic_update_slice x0 -> x8, local copies, waits for them, and re-layouts: none -> 17.4 us  [the longest x4 8.07 us: collect(): lax.dynamic_update_slice_in_dim(out, from_left, (index - hop) % count * s...]
    ppermute x0 -> x7, starting transfers between devices: none -> 8.98 us  [the longest x3 8.96 us: collect(): from_right = lax.ppermute(from_right, axis, left)]
    broadcast_in_dim x0 -> x1, local copies, waits for them, and re-layouts: none -> 5.46 us  [collect(): jnp.zeros((*shard.shape[:dim], count * span, *shard.shape[dim + 1:]), sha...]
    unnamed x15 -> x23, local copies, waits for them, and re-layouts: 15.9 us -> 15.6 us
  transfers between devices with their start and end apart: 4 -> 10, of which waited for: 4 -> 5; matrix products, arithmetic and copies ran while one was open for 2% -> 8% of each run, Pallas kernels for 0% -> 0%
where the time goes in v1:
time: 357 us
  waiting for transfers between devices  173 us (48%)
  blocking collectives  101 us (28%)
  local copies, waits for them, and re-layouts  41.8 us (12%)
  matrix products  16.7 us (5%)
  between operations  15.3 us (4%)
  starting transfers between devices  9.1 us (3%)
    reduce_scatter x1, waiting for transfers between devices, body(): lax.psum_scatter(image_gradient_total, 'segment', scatter_dimension=1, ti...  89.3 us
    psum x1, blocking collectives, body(): down_sum, up_sum = lax.psum((grad_down, up_gradient), 'dp')  51.2 us
    all_gather x1, waiting for transfers between devices, body(): lax.all_gather(encoder_image_states, 'segment', axis=1, tiled=True)  34.2 us
    psum x1, blocking collectives, body(): lax.psum(jnp.dot(image_fourth, adapter_down_weight[0], preferred_element_...  25.9 us
    ppermute x4, waiting for transfers between devices, collect(): from_left = lax.ppermute(from_left, axis, upward)  25.2 us
    psum x1, blocking collectives, body(): backward_lowrank = lax.psum(backward_piece, 'mp').astype(jnp.bfloat16)  23.9 us
    psum x1, waiting for transfers between devices, body(): result = lax.psum(shared_sum, 'mp')  23.3 us
    unnamed x23, local copies, waits for them, and re-layouts  15.6 us
  transfers between devices with their start and end apart: 10, of which 5 were waited for; matrix products, arithmetic and copies ran while one was open for 8% of the time, Pallas kernels for 0%

profile of v1, /device:TPU:2, one launch (start us, length us, event | category | flops | bytes accessed | tf_op | source)
XLA Modules:
  0.0 356.8 jit_solution(10266128619672944551)
XLA Ops:
  8.0 2.9 collective-permute-start.1
  10.9 12.7 %collective-permute-done = bf16[1024,2,256]{2,1,0:T(2,128)(2,1)S(1)} collective-permute-done((bf16[1024,2,256]{2,1,0:T(2,128)(2,1)}, bf16[1024,2,256]{2,1,0:T(2,128)(2,1)S(1)}, u32[]{:S(2)}, u32[]{:S(2)}) %collective-permute-start) | collective-permute-done | bytes 1048608 | tf_op jit(solution)/shard_map/ppermute | solution.py:22
  23.6 3.1 collective-permute-start.3
  26.7 12.5 %collective-permute-done.2 = bf16[1024,2,256]{2,1,0:T(2,128)(2,1)} collective-permute-done((bf16[1024,2,256]{2,1,0:T(2,128)(2,1)S(1)}, bf16[1024,2,256]{2,1,0:T(2,128)(2,1)}, u32[]{:S(2)}, u32[]{:S(2)}) %collective-permute-start.2) | collective-permute-done | bytes 1048608 | tf_op jit(solution)/shard_map/ppermute | solution.py:22
  39.2 1.3 copy.33
  41.1 2.1 copy.34
  43.9 3.0 collective-permute-start.5
  46.9 5.5 %broadcast_in_dim.19 = bf16[8192,2,256]{2,1,0:T(2,128)(2,1)} broadcast(bf16[]{:T(256)} %constant.69.clone.1), dimensions={} | broadcast | bytes 8388610 | tf_op jit(solution)/shard_map/broadcast_in_dim | solution.py:17
  52.4 1.7 constant_dynamic-update-slice_fusion.7
  54.0 1.7 constant_dynamic-update-slice_fusion.6
  55.8 3.0 constant_dynamic-update-slice_fusion.5
  58.7 2.9 constant_dynamic-update-slice_fusion.4
  61.7 2.9 constant_dynamic-update-slice_fusion.3
  64.6 1.7 constant_dynamic-update-slice_fusion.2
  66.3 1.7 constant_dynamic-update-slice_fusion.1
  68.1 34.2 %all-gather.2.cloned.1.call-done = bf16[1,128,8192]{2,1,0:T(8,128)(2,1)} async-done(((bf16[1,8,8192]{2,1,0:T(8,128)(2,1)}), bf16[1,128,8192]{2,1,0:T(8,128)(2,1)}) %all-gather.2.cloned.1.call-update) | async-done | bytes 2097168 | tf_op jit(solution)/shard_map/all_gather | solution.py:46
  102.2 1.3 fusion.24
  103.6 25.9 %psum.35 = bf16[128,128]{1,0:T(8,128)(2,1)S(1)} all-reduce(f32[128,128]{1,0:T(8,128)S(1)} %fusion.24), channel_id=1, replica_groups=mesh['segment'=16,'dp'=8,'mp'=4] {'mp'}, use_global_device_ids=true, to_apply=%region_0.0 | all-reduce | flops 16384 | bytes 98304 | tf_op jit(solution)/shard_map/psum | solution.py:55
  130.0 1.7 constant_dynamic-update-slice_fusion
  131.7 8.2 %copy.35 = bf16[1024,8,2,256]{3,1,2,0:T(8,128)(2,1)} copy(bf16[1024,8,2,256]{3,2,1,0:T(2,128)(2,1)} %bitcast.52) | data formatting | bytes 16777216
  139.8 5.8 %fusion.13 = bf16[128,512]{0,1:T(8,128)(2,1)S(1)} fusion(bf16[8192,512]{1,0:T(8,128)(2,1)} %bitcast.125, bf16[1,128,8192]{2,1,0:T(8,128)(2,1)S(1)} %copy-done.5, f32[128,256]{0,1:T(8,128)S(1)} %fusion.43, f32[128,256]{0,1:T(8,128)S(1)} %fusion.47), kind=kOutput, calls=%fused_computation.12 | convolution fusion | flops 1074003968 | bytes 10878976 | tf_op jit(solution)/shard_map/dot_general | solution.py:75
  148.2 1.4 slice-done.1
  149.7 2.8 fusion.37
  152.6 1.8 copy-done.1
  154.5 1.9 copy.46
  156.4 23.9 %psum.36 = bf16[128,128]{0,1:T(8,128)(2,1)S(1)} all-reduce(f32[128,128]{0,1:T(8,128)S(1)} %maximum_multiply_fusion.2), channel_id=1, replica_groups=mesh['segment'=16,'dp'=8,'mp'=4] {'mp'}, use_global_device_ids=true, to_apply=%region_4.5 | all-reduce | flops 16384 | bytes 98304 | tf_op jit(solution)/shard_map/psum | solution.py:133
  180.3 2.5 fusion.1
  183.4 1.4 fusion.26
  184.8 89.3 %reduce-scatter.2.cloned.1.call-done = f32[1,8,8192]{2,1,0:T(8,128)} async-done(((f32[1,128,8192]{2,1,0:T(8,128)}), f32[1,8,8192]{2,1,0:T(8,128)}) %reduce-scatter.2.cloned.1.call-update) | async-done | bytes 262160 | tf_op jit(solution)/shard_map/reduce_scatter | solution.py:170
  274.1 51.2 %all-reduce.5 = (bf16[2048,128]{1,0:T(8,128)(2,1)}, bf16[2,64,256]{2,1,0:T(8,128)(2,1)}) all-reduce(f32[2048,128]{1,0:T(8,128)S(1)} %fusion.26, f32[2,64,256]{2,1,0:T(8,128)S(1)} %maximum_multiply_fusion.1), channel_id=1, replica_groups=mesh['segment'=16,'dp'=8,'mp'=4] {'dp'}, use_global_device_ids=true, to_apply=%region_5.6 | all-reduce | flops 294912 | bytes 1769472 | tf_op jit(solution)/shard_map/psum | solution.py:153
  325.3 23.3 %all-reduce.4.cloned.1.call-done = f32[1,8,8192]{2,1,0:T(8,128)} async-done(((f32[1,8,8192]{2,1,0:T(8,128)}), f32[1,8,8192]{2,1,0:T(8,128)}) %all-reduce.4.cloned.1.call-update) | async-done | bytes 262160 | tf_op jit(solution)/shard_map/psum | solution.py:171
  348.6 1.7 copy.52
  (50 shorter events, 4.5 us)
Async XLA Ops:
  7.2 95.1 %copy-start = (bf16[1,2048,128]{2,1,0:T(8,128)(2,1)S(1)}, bf16[1,2048,128]{2,1,0:T(8,128)(2,1)}, u32[]{:S(2)}) copy-start(bf16[1,2048,128]{2,1,0:T(8,128)(2,1)} %param.10) | copy-start | bytes 1572868
  7.2 45.2 %copy-start.2 = (bf16[1,1024,2,256]{3,2,1,0:T(2,128)(2,1)S(1)}, bf16[1,1024,2,256]{3,2,1,0:T(2,128)(2,1)}, u32[]{:S(2)}) copy-start(bf16[1,1024,2,256]{3,2,1,0:T(2,128)(2,1)} %param.9) | copy-start | bytes 3145732
  7.2 95.0 %all-gather.2.cloned.1.call-start = ((), (), s32[]{:S(2)}) async-start(), calls=%async_computation.1 | async-start | bytes 2228224 | tf_op jit(solution)/shard_map/all_gather | solution.py:46
  7.9 266.1 %reduce-scatter.2.cloned.1.call-start = ((), (), s32[]{:S(2)}) async-start(), calls=%async_computation.2 | async-start | bytes 4456448 | tf_op jit(solution)/shard_map/reduce_scatter | solution.py:170
  8.0 15.7 %collective-permute-start = (bf16[1024,2,256]{2,1,0:T(2,128)(2,1)}, bf16[1024,2,256]{2,1,0:T(2,128)(2,1)S(1)}, u32[]{:S(2)}, u32[]{:S(2)}) collective-permute-start(bf16[1024,2,256]{2,1,0:T(2,128)(2,1)} %bitcast.132), channel_id=1, source_target_pairs={{0,4},{4,8},{8,12},{12,16},{16,20},{20,24},{24,28},{28,0},{1,5},{5... | collective-permute-start | bytes 3145736 | tf_op jit(solution)/shard_map/ppermute | solution.py:22
  8.0 15.6 %collective-permute-start.1 = (bf16[1024,2,256]{2,1,0:T(2,128)(2,1)}, bf16[1024,2,256]{2,1,0:T(2,128)(2,1)}, u32[]{:S(2)}, u32[]{:S(2)}) collective-permute-start(bf16[1024,2,256]{2,1,0:T(2,128)(2,1)} %bitcast.133), channel_id=1, source_target_pairs={{0,28},{4,0},{8,4},{12,8},{16,12},{20,16},{24,20},{28,24},{1,29},{... | collective-permute-start | bytes 3145736 | tf_op jit(solution)/shard_map/ppermute | solution.py:27
  23.6 3.1 copy-start.3
  23.6 15.5 %collective-permute-start.2 = (bf16[1024,2,256]{2,1,0:T(2,128)(2,1)S(1)}, bf16[1024,2,256]{2,1,0:T(2,128)(2,1)}, u32[]{:S(2)}, u32[]{:S(2)}) collective-permute-start(bf16[1024,2,256]{2,1,0:T(2,128)(2,1)S(1)} %collective-permute-done), channel_id=1, source_target_pairs={{0,4},{4,8},{8,12},{12,16},{16,20},{20,24},{24,28},{28,0},{1,5},{5... | collective-permute-start | bytes 3145736 | tf_op jit(solution)/shard_map/ppermute | solution.py:22
  23.6 20.3 %collective-permute-start.3 = (bf16[1024,2,256]{2,1,0:T(2,128)(2,1)}, bf16[1024,2,256]{2,1,0:T(2,128)(2,1)}, u32[]{:S(2)}, u32[]{:S(2)}) collective-permute-start(bf16[1024,2,256]{2,1,0:T(2,128)(2,1)} %collective-permute-done.1), channel_id=1, source_target_pairs={{0,28},{4,0},{8,4},{12,8},{16,12},{20,16},{24,20},{28,24},{1,29},{... | collective-permute-start | bytes 3145736 | tf_op jit(solution)/shard_map/ppermute | solution.py:27
  39.2 22.5 %collective-permute-start.4 = (bf16[1024,2,256]{2,1,0:T(2,128)(2,1)}, bf16[1024,2,256]{2,1,0:T(2,128)(2,1)S(1)}, u32[]{:S(2)}, u32[]{:S(2)}) collective-permute-start(bf16[1024,2,256]{2,1,0:T(2,128)(2,1)} %collective-permute-done.2), channel_id=1, source_target_pairs={{0,4},{4,8},{8,12},{12,16},{16,20},{20,24},{24,28},{28,0},{1,5},{5... | collective-permute-start | bytes 3145736 | tf_op jit(solution)/shard_map/ppermute | solution.py:22
  43.9 10.2 %copy-start.4 = (bf16[1024,2,256]{2,1,0:T(2,128)(2,1)S(1)}, bf16[1024,2,256]{2,1,0:T(2,128)(2,1)}, u32[]{:S(2)}) copy-start(bf16[1024,2,256]{2,1,0:T(2,128)(2,1)} %copy-done.3) | copy-start | bytes 3145732
  43.9 22.4 %collective-permute-start.5 = (bf16[1024,2,256]{2,1,0:T(2,128)(2,1)}, bf16[1024,2,256]{2,1,0:T(2,128)(2,1)S(1)}, u32[]{:S(2)}, u32[]{:S(2)}) collective-permute-start(bf16[1024,2,256]{2,1,0:T(2,128)(2,1)} %collective-permute-done.3), channel_id=1, source_target_pairs={{0,28},{4,0},{8,4},{12,8},{16,12},{20,16},{24,20},{28,24},{1,29},{... | collective-permute-start | bytes 3145736 | tf_op jit(solution)/shard_map/ppermute | solution.py:27
  52.4 77.1 %copy-start.7 = (bf16[1,2,64,256]{3,2,1,0:T(8,128)(2,1)S(1)}, bf16[1,2,64,256]{3,2,1,0:T(8,128)(2,1)}, u32[]{:S(2)}) copy-start(bf16[1,2,64,256]{3,2,1,0:T(8,128)(2,1)} %param.11) | copy-start | bytes 196612
  61.7 68.3 %collective-permute-start.6 = (bf16[1024,2,256]{2,1,0:T(2,128)(2,1)S(1)}, bf16[1024,2,256]{2,1,0:T(2,128)(2,1)S(1)}, u32[]{:S(2)}, u32[]{:S(2)}) collective-permute-start(bf16[1024,2,256]{2,1,0:T(2,128)(2,1)S(1)} %collective-permute-done.4), channel_id=1, source_target_pairs={{0,4},{4,8},{8,12},{12,16},{16,20},{20,24},{24,28},{28,0},{1,5},{5... | collective-permute-start | bytes 3145736 | tf_op jit(solution)/shard_map/ppermute | solution.py:22
  131.7 8.2 %copy-start.5 = (bf16[1,128,8192]{2,1,0:T(8,128)(2,1)S(1)}, bf16[1,128,8192]{2,1,0:T(8,128)(2,1)}, u32[]{:S(2)}) copy-start(bf16[1,128,8192]{2,1,0:T(8,128)(2,1)} %all-gather.2.cloned.1.call-done) | copy-start | bytes 6291460
  139.8 6.4 %copy-start.6 = (bf16[1,1,128,2048]{2,3,1,0:T(8,128)(2,1)S(1)}, bf16[1,1,128,2048]{2,3,1,0:T(8,128)(2,1)}, u32[]{:S(2)}) copy-start(bf16[1,1,128,2048]{2,3,1,0:T(8,128)(2,1)} %copy.34) | copy-start | bytes 1572868
  146.1 2.2 slice-start
  146.6 3.0 slice-start.1
  152.5 2.0 copy-start.1
  182.9 165.7 %all-reduce.4.cloned.1.call-start = ((), (), s32[]{:S(2)}) async-start(), calls=%async_computation.3 | async-start | bytes 524288 | tf_op jit(solution)/shard_map/psum | solution.py:171
Sparse Core Ops, SparseCore 0:
  10.1 92.1 all-gather.1
  183.0 90.9 reduce-scatter.1
  277.0 71.5 all-reduce.3
